TPU v7x, 128 devices: a whole 4x4x4 slice. The times are simulated.
128 devices in a mesh: frames: 16 (over x, y_lo, core), pairs: 8 (over y_hi, z).
Axes of the slice: x: 4, y: 4 (y_hi: 2, y_lo: 2; y = y_hi * 2 + y_lo), z: 4, core: 2. Of those that a mesh axis runs over, the one named last changes fastest.
Arguments:
- coords: float32 [8192, 3, 384], P('frames'), may hold values from -3 to 3
- pair_first: int32 [512], P('pairs'), may hold values from 0 to 383
- pair_second: int32 [65536], P('pairs'), may hold values from 0 to 383
- enc_weight: bfloat16 [64, 65536], P(None, 'pairs'), may hold values from -0.0234375 to 0.0234375
- enc_bias: float32 [64], replicated, may hold values from -4 to 4
- dec_weight: bfloat16 [64, 65536], P(None, 'pairs'), may hold values from -0.75 to 0.75
- dec_bias: float32 [65536], P('pairs'), may hold values from -3 to 3
- lag_frames: int32 [1], replicated, may hold values from 256 to 512
Outputs:
- grad_enc: float32 [64, 65536], P(None, 'pairs')
- grad_dec: float32 [64, 65536], P(None, 'pairs')
Inputs may be any that keep to these rules, and one draw needn't show every extreme that they name: Residue numbers; pair p joins residue pair_first[p // 128] with residue pair_second[p].
All inputs are finite; a program needn't handle non-finite values.
Results may differ from a plain program's by a relative error of at most 0.0003.
Values may be sent and summed in bfloat16 or wider, within the bound.
No kernel may reach another device: no remote copies, remote signals or barrier semaphores. Data moves between devices by JAX's collectives and lax.ppermute only.
A program may use at most 192 MiB of HBM per device.

v0:
```python
from functools import partial
import jax
import jax.numpy as jnp
from jax import lax
from jax.sharding import PartitionSpec as P

cutoff_dist = 2.3
softness = 0.4


def from_behind(block, axis, distance):
    devices = range(lax.axis_size(axis))
    route = [(i - distance, i) for i in devices if i - distance in devices]
    return lax.ppermute(block, axis, route)


def contact_rows(frame_block, first_res, second):
    near = jnp.take(frame_block, first_res, axis=2)
    far = jnp.take(frame_block, second, axis=2)
    far = far.reshape(far.shape[0], 3, first_res.shape[0], 128)
    offset = far - near[..., None]
    distance = jnp.sqrt(jnp.sum(offset * offset, axis=1))
    value = jax.nn.sigmoid((cutoff_dist - distance) / softness)
    return value.reshape(frame_block.shape[0], -1).astype(jnp.bfloat16)


def all_contacts(coords, first_res, second):
    frame_rows = coords.shape[0]
    block_rows = min(128, frame_rows)
    grouped = coords.reshape(frame_rows // block_rows, block_rows, coords.shape[1], coords.shape[2])
    result = lax.map(partial(contact_rows, first_res=first_res, second=second), grouped)
    return result.reshape(frame_rows, -1)


def later_rows(own, following, row_ids, frame_rows):
    own_part = jnp.take(own, jnp.minimum(row_ids, frame_rows - 1), axis=0)
    next_part = jnp.take(following, jnp.maximum(row_ids - frame_rows, 0), axis=0)
    inside = (row_ids < frame_rows).reshape((-1,) + (1,) * (own.ndim - 1))
    return jnp.where(inside, own_part, next_part)


def local(coords, pair_first, pair_second, enc_weight, enc_bias, dec_weight, dec_bias, lag_frames):
    frame_rows = coords.shape[0]
    total_frames = frame_rows * lax.axis_size("frames")
    shift_now = lag_frames[0]
    own_contacts = all_contacts(coords, pair_first, pair_second)
    following = from_behind(own_contacts, "frames", -1)
    partial_sum = lax.dot_general(
        enc_weight, own_contacts, (((1,), (1,)), ((), ())), preferred_element_type=jnp.float32
    )
    latent = jnp.tanh(lax.psum(partial_sum, "pairs") + enc_bias[:, None])
    latent_bf = latent.astype(jnp.bfloat16)
    scale_factor = 1.0 / jnp.sqrt(jnp.float32(total_frames) - shift_now.astype(jnp.float32))
    block_rows = min(512, frame_rows)
    block_count = frame_rows // block_rows
    first_frame = lax.axis_index("frames") * frame_rows

    def decode_block(grad_sum, block_idx):
        begin_row = block_idx * block_rows
        local_ids = begin_row + jnp.arange(block_rows, dtype=jnp.int32)
        row_ids = local_ids + shift_now
        target = later_rows(own_contacts, following, row_ids, frame_rows)
        decoded = (
            lax.dot_general(
                latent_bf, dec_weight, (((0,), (0,)), ((), ())), preferred_element_type=jnp.float32
            )
            + dec_bias[None, :]
        )
        usable = first_frame + local_ids + shift_now < total_frames
        err_bf = jnp.where(
            usable[:, None], (decoded - target.astype(jnp.float32)) * scale_factor, 0.0
        ).astype(jnp.bfloat16)
        grad_sum = grad_sum + jnp.dot(latent_bf, err_bf, preferred_element_type=jnp.float32)
        back_block = lax.dot_general(
            dec_weight, err_bf, (((1,), (1,)), ((), ())), preferred_element_type=jnp.float32
        )
        return (grad_sum, back_block)

    zeros = jnp.zeros((latent.shape[0], dec_weight.shape[1]), jnp.float32)
    grad_dec, back_blocks = lax.scan(decode_block, zeros, jnp.arange(block_count, dtype=jnp.int32))
    back_terms = jnp.transpose(back_blocks, (1, 0, 2)).reshape(latent.shape[0], frame_rows)
    backward = lax.psum(back_terms, "pairs")
    hidden_bf = (backward * (1.0 - latent * latent)).astype(jnp.bfloat16)
    grad_enc = jnp.dot(hidden_bf, own_contacts, preferred_element_type=jnp.float32)
    grad_dec, grad_enc = lax.psum((grad_dec, grad_enc), "frames")
    return (grad_enc, grad_dec)


def solution(mesh):
    placed = (
        P("frames", None, None),
        P("pairs"),
        P("pairs"),
        P(None, "pairs"),
        P(),
        P(None, "pairs"),
        P("pairs"),
        P(),
    )
    return jax.shard_map(
        local,
        mesh=mesh,
        in_specs=placed,
        out_specs=(P(None, "pairs"), P(None, "pairs")),
        check_vma=False,
    )
```

profile of v0, /device:TPU:0, one launch (start us, length us, event | category | flops | bytes accessed | tf_op | source)
XLA Modules:
  0.0 823.3 jit_solution(3909381968403380009)
XLA Ops:
  7.2 363.3 %while.2 = (s32[]{:T(128)}, bf16[4,128,8192]{2,1,0:T(8,128)(2,1)}, s32[8192]{0:T(1024)}, f32[4,128,3,384]{3,1,0,2:T(8,128)}, s32[64]{0:T(128)}, /*index=5*/s32[]{:T(128)}) while((s32[]{:T(128)}, bf16[4,128,8192]{2,1,0:T(8,128)(2,1)}, s32[8192]{0:T(1024)}, f32[4,128,3,384]{3,1,0,2:T(8,128)}, s32[64]{0:T(128)}, /*index=5*/s32[]{:T(128)}) %tuple.40), condition=%wide.region_2.3_spmd, body=%wide.region_0.2_spmd.sunk | while | flops 17933888 | bytes 85054936 | solution.py:31
  9.4 0.8 compare_select_fusion.6
  10.2 1.1 constant_dynamic-slice_fusion.2
  12.5 59.9 %gather_fusion = f32[8192,128,3]{1,2,0:T(4,128)} fusion(f32[128,3,384]{0,1,2:T(4,128)S(1)} %bitcast.54, s32[8192]{0:T(1024)S(1)} %broadcast_clamp_fusion.2), kind=kCustom, calls=%fused_computation.clone.1 | custom fusion | bytes 25198592 | tf_op jit(solution)/shard_map/while/body/eval_jaxpr/jit(_take)/gather | solution.py:19
  72.4 11.1 %copy.28 = f32[128,3,8192]{0,2,1:T(8,128)} copy(f32[128,3,8192]{0,1,2:T(4,128)} %bitcast.55) | data formatting | bytes 25165824 | tf_op jit(solution)/shard_map/while/body/eval_jaxpr/jit(_take)/gather | solution.py:19
  83.5 6.6 multiply_reduce_fusion.2
  90.1 2.0 divide_convert_fusion.2
  92.1 2.9 copy.30
  95.0 3.1 constant_dynamic-update-slice_fusion.2
  100.3 0.8 compare_select_fusion.6
  101.1 1.1 constant_dynamic-slice_fusion.2
  103.3 59.9 %gather_fusion = f32[8192,128,3]{1,2,0:T(4,128)} fusion(f32[128,3,384]{0,1,2:T(4,128)S(1)} %bitcast.54, s32[8192]{0:T(1024)S(1)} %broadcast_clamp_fusion.2), kind=kCustom, calls=%fused_computation.clone.1 | custom fusion | bytes 25198592 | tf_op jit(solution)/shard_map/while/body/eval_jaxpr/jit(_take)/gather | solution.py:19
  163.2 11.1 %copy.28 = f32[128,3,8192]{0,2,1:T(8,128)} copy(f32[128,3,8192]{0,1,2:T(4,128)} %bitcast.55) | data formatting | bytes 25165824 | tf_op jit(solution)/shard_map/while/body/eval_jaxpr/jit(_take)/gather | solution.py:19
  174.3 6.6 multiply_reduce_fusion.2
  180.9 2.0 divide_convert_fusion.2
  183.0 2.9 copy.30
  185.9 3.1 constant_dynamic-update-slice_fusion.2
  191.0 0.8 compare_select_fusion.6
  191.9 1.1 constant_dynamic-slice_fusion.2
  194.1 59.9 %gather_fusion = f32[8192,128,3]{1,2,0:T(4,128)} fusion(f32[128,3,384]{0,1,2:T(4,128)S(1)} %bitcast.54, s32[8192]{0:T(1024)S(1)} %broadcast_clamp_fusion.2), kind=kCustom, calls=%fused_computation.clone.1 | custom fusion | bytes 25198592 | tf_op jit(solution)/shard_map/while/body/eval_jaxpr/jit(_take)/gather | solution.py:19
  254.0 11.1 %copy.28 = f32[128,3,8192]{0,2,1:T(8,128)} copy(f32[128,3,8192]{0,1,2:T(4,128)} %bitcast.55) | data formatting | bytes 25165824 | tf_op jit(solution)/shard_map/while/body/eval_jaxpr/jit(_take)/gather | solution.py:19
  265.1 6.6 multiply_reduce_fusion.2
  271.7 2.0 divide_convert_fusion.2
  273.7 2.9 copy.30
  276.6 3.1 constant_dynamic-update-slice_fusion.2
  281.9 0.8 compare_select_fusion.6
  282.7 1.1 constant_dynamic-slice_fusion.2
  284.9 59.9 %gather_fusion = f32[8192,128,3]{1,2,0:T(4,128)} fusion(f32[128,3,384]{0,1,2:T(4,128)S(1)} %bitcast.54, s32[8192]{0:T(1024)S(1)} %broadcast_clamp_fusion.2), kind=kCustom, calls=%fused_computation.clone.1 | custom fusion | bytes 25198592 | tf_op jit(solution)/shard_map/while/body/eval_jaxpr/jit(_take)/gather | solution.py:19
  344.8 11.1 %copy.28 = f32[128,3,8192]{0,2,1:T(8,128)} copy(f32[128,3,8192]{0,1,2:T(4,128)} %bitcast.55) | data formatting | bytes 25165824 | tf_op jit(solution)/shard_map/while/body/eval_jaxpr/jit(_take)/gather | solution.py:19
  355.9 6.6 multiply_reduce_fusion.2
  362.5 2.0 divide_convert_fusion.2
  364.6 2.9 copy.30
  367.5 3.1 constant_dynamic-update-slice_fusion.2
  370.5 1.3 collective-permute-start
  371.8 6.9 convolution_bitcast_fusion.1
  379.8 19.9 %gather_fusion.2 = bf16[512,8192]{1,0:T(8,128)(2,1)} fusion(bf16[512,8192]{1,0:T(8,128)(2,1)} %bitcast.59, s32[1024]{0:T(1024)S(1)} %pad_clamp_fusion.2), kind=kCustom, calls=%fused_computation.2.clone | custom fusion | bytes 16779264 | tf_op jit(solution)/shard_map/while/body/eval_jaxpr/jit(_take)/gather | solution.py:36
  399.7 142.4 %all-reduce.5.cloned.1.call-done = f32[64,512]{1,0:T(8,128)} async-done(((f32[64,512]{1,0:T(8,128)}), f32[64,512]{1,0:T(8,128)}) %all-reduce.5.cloned.1.call-update) | async-done | bytes 131088 | tf_op jit(solution)/shard_map/psum | solution.py:51
  542.2 9.1 %fusion.9 = f32[512,8192]{1,0:T(8,128)} fusion(bf16[64,8192]{1,0:T(8,128)(2,1)S(1)} %copy-done, f32[64,512]{1,0:T(8,128)} %all-reduce.5.cloned.1.call-done, f32[64]{0:T(128)S(1)} %copy-done.4), kind=kOutput, calls=%fused_computation.39 | convolution fusion | flops 536936448 | bytes 17957120 | tf_op jit(solution)/shard_map/while/body/eval_jaxpr/dot_general | solution.py:64
  551.2 20.1 %gather_fusion.3 = bf16[512,8192]{1,0:T(8,128)(2,1)} fusion(bf16[512,8192]{1,0:T(8,128)(2,1)} %collective-permute-done, s32[1024]{0:T(1024)S(1)} %pad_clamp_fusion.1), kind=kCustom, calls=%fused_computation.3.clone | custom fusion | bytes 16779264 | tf_op jit(solution)/shard_map/while/body/eval_jaxpr/jit(_take)/gather | solution.py:37
  571.4 14.2 %select_convert_fusion = bf16[512,8192]{1,0:T(8,128)(2,1)S(1)} fusion(f32[512,8192]{1,0:T(8,128)} %fusion.9, bf16[512,8192]{1,0:T(8,128)(2,1)} %gather_fusion.3, bf16[512,8192]{1,0:T(8,128)(2,1)} %gather_fusion.2, f32[]{:T(128)S(6)} %sqrt.15, f32[8192]{0:T(1024)S(1)} %copy-done.3, pred[512]{0:T(512)(128)(4,1)S(1)} %get-tuple-element.89, ...), kind=kLoop, calls=%fused_computation.18 | loop fusion | flops 37748736 | bytes 41977860 | tf_op jit(solution)/shard_map/while/body/eval_jaxpr/convert_element_type | solution.py:72
  585.6 3.2 copy-done.1
  588.8 3.3 convolution_bitcast_fusion
  592.4 6.3 fusion.7
  598.8 76.2 %all-reduce.7.cloned.1.call-done = f32[64,512]{1,0:T(8,128)} async-done(((f32[64,512]{1,0:T(8,128)}), f32[64,512]{1,0:T(8,128)}) %all-reduce.7.cloned.1.call-update) | async-done | bytes 131088 | tf_op jit(solution)/shard_map/psum | solution.py:82
  675.0 6.4 fusion.2
  681.4 129.2 %all-reduce.9.cloned.1.call-done = (f32[64,8192]{1,0:T(8,128)}, f32[64,8192]{1,0:T(8,128)}) async-done(((f32[64,8192]{1,0:T(8,128)}, f32[64,8192]{1,0:T(8,128)}), (f32[64,8192]{1,0:T(8,128)}, f32[64,8192]{1,0:T(8,128)})) %all-reduce.9.cloned.1.call-update) | async-done | bytes 4194320 | tf_op jit(solution)/shard_map/psum | solution.py:85
  810.6 3.1 copy.45
  813.7 3.1 copy.46
  (59 shorter events, 13.6 us)
Async XLA Ops:
  7.2 535.0 %copy-start = (bf16[64,8192]{1,0:T(8,128)(2,1)S(1)}, bf16[64,8192]{1,0:T(8,128)(2,1)}, u32[]{:S(2)}) copy-start(bf16[64,8192]{1,0:T(8,128)(2,1)} %param.17) | copy-start | bytes 3145732
  7.2 535.0 %all-reduce.5.cloned.1.call-start = ((), (), s32[]{:S(2)}) async-start(), calls=%async_computation | async-start | bytes 262144 | tf_op jit(solution)/shard_map/psum | solution.py:51
  370.5 180.7 %collective-permute-start = (bf16[512,8192]{1,0:T(8,128)(2,1)}, bf16[512,8192]{1,0:T(8,128)(2,1)}, u32[]{:S(2)}, u32[]{:S(2)}) collective-permute-start(bf16[512,8192]{1,0:T(8,128)(2,1)} %bitcast.57), channel_id=1, source_target_pairs={{8,0},{16,8},{24,16},{32,24},{40,32},{48,40},{56,48},{64,56},{72,6... | collective-permute-start | bytes 25165832 | tf_op jit(solution)/shard_map/ppermute | solution.py:14
  378.8 296.2 %all-reduce.7.cloned.1.call-start = ((), (), s32[]{:S(2)}) async-start(), calls=%async_computation.1 | async-start | bytes 262144 | tf_op jit(solution)/shard_map/psum | solution.py:82
  379.8 162.4 %copy-start.4 = (f32[64]{0:T(128)S(1)}, f32[64]{0:T(128)}, u32[]{:S(2)}) copy-start(f32[64]{0:T(128)} %param.16) | copy-start | bytes 772
  551.2 20.1 %copy-start.3 = (f32[8192]{0:T(1024)S(1)}, f32[8192]{0:T(1024)}, u32[]{:S(2)}) copy-start(f32[8192]{0:T(1024)} %param.18) | copy-start | bytes 98308
  585.5 3.2 copy-start.1
  588.8 3.7 copy-start.2
  592.1 218.5 %all-reduce.9.cloned.1.call-start = ((), (), s32[]{:S(2)}) async-start(), calls=%async_computation.2 | async-start | bytes 8388608 | tf_op jit(solution)/shard_map/psum | solution.py:85
Sparse Core Ops, SparseCore 0:
  378.9 163.2 all-reduce.4
  592.2 82.6 all-reduce.6
  681.5 129.0 all-reduce.8
where the time goes:
time: 825 us; the launch traced here: 823 us
  local copies, waits for them, and re-layouts  366 us (44%)
  waiting for transfers between devices  348 us (42%)
  other arithmetic  60.8 us (7%)
  matrix products  32.1 us (4%)
  between operations  14.5 us (2%)
    gather x8, local copies, waits for them, and re-layouts, contact_rows(): far = jnp.take(frame_block, second, axis=2)  284 us
    psum x1, waiting for transfers between devices, local(): latent = jnp.tanh(lax.psum(partial_sum, 'pairs') + enc_bias[:, None])  142 us
    psum x1, waiting for transfers between devices, local(): grad_dec, grad_enc = lax.psum((grad_dec, grad_enc), 'frames')  129 us
    psum x1, waiting for transfers between devices, local(): backward = lax.psum(back_terms, 'pairs')  76.2 us
    reduce_sum x4, other arithmetic, contact_rows(): distance = jnp.sqrt(jnp.sum(offset * offset, axis=1))  26.4 us
    dynamic_update_slice x8, local copies, waits for them, and re-layouts, all_contacts(): lax.map(partial(contact_rows, first_res=first_res, second=second), grouped)  24 us
    gather x1, local copies, waits for them, and re-layouts, later_rows(): jnp.take(following, jnp.maximum(row_ids - frame_rows, 0), axis=0)  20.1 us
    gather x1, local copies, waits for them, and re-layouts, later_rows(): own_part = jnp.take(own, jnp.minimum(row_ids, frame_rows - 1), axis=0)  19.9 us
  transfers between devices with their start and end apart: 4, of which 3 were waited for; matrix products, arithmetic and copies ran while one was open for 5% of the time, Pallas kernels for 0%

commit v1 on v0

--- a/solution.py
+++ b/solution.py
@@ -1,3 +1,4 @@
+import functools
 from functools import partial
 import jax
 import jax.numpy as jnp
@@ -6,6 +7,13 @@
 
 cutoff_dist = 2.3
 softness = 0.4
+
+
+def _spread_sample(content, link_axis):
+    return jnp.sum(lax.all_gather(content, link_axis), axis=0)
+
+
+change_patches_up = functools.partial(_spread_sample, link_axis="pairs")
 
 
 def from_behind(block, axis, distance):
@@ -79,7 +87,7 @@
     zeros = jnp.zeros((latent.shape[0], dec_weight.shape[1]), jnp.float32)
     grad_dec, back_blocks = lax.scan(decode_block, zeros, jnp.arange(block_count, dtype=jnp.int32))
     back_terms = jnp.transpose(back_blocks, (1, 0, 2)).reshape(latent.shape[0], frame_rows)
-    backward = lax.psum(back_terms, "pairs")
+    backward = change_patches_up(back_terms)
     hidden_bf = (backward * (1.0 - latent * latent)).astype(jnp.bfloat16)
     grad_enc = jnp.dot(hidden_bf, own_contacts, preferred_element_type=jnp.float32)
     grad_dec, grad_enc = lax.psum((grad_dec, grad_enc), "frames")

time: 825 us -> 789 us (0.956)
  waiting for transfers between devices: 348 us -> 310 us
    psum x1 -> x0, waiting for transfers between devices: 76.2 us -> none  [local(): backward = lax.psum(back_terms, 'pairs')]
    all_gather x0 -> x1, waiting for transfers between devices: none -> 37.8 us  [_spread_sample(): return jnp.sum(lax.all_gather(content, link_axis), axis=0)]
where the time goes in v1:
time: 789 us; the launch traced here: 787 us
  local copies, waits for them, and re-layouts  366 us (46%)
  waiting for transfers between devices  310 us (39%)
  other arithmetic  62.1 us (8%)
  matrix products  32 us (4%)
  between operations  14.5 us (2%)
    gather x8, local copies, waits for them, and re-layouts, contact_rows(): far = jnp.take(frame_block, second, axis=2)  284 us
    psum x1, waiting for transfers between devices, local(): latent = jnp.tanh(lax.psum(partial_sum, 'pairs') + enc_bias[:, None])  142 us
    psum x1, waiting for transfers between devices, local(): grad_dec, grad_enc = lax.psum((grad_dec, grad_enc), 'frames')  130 us
    all_gather x1, waiting for transfers between devices, _spread_sample(): return jnp.sum(lax.all_gather(content, link_axis), axis=0)  37.8 us
    reduce_sum x4, other arithmetic, contact_rows(): distance = jnp.sqrt(jnp.sum(offset * offset, axis=1))  26.4 us
    dynamic_update_slice x8, local copies, waits for them, and re-layouts, all_contacts(): lax.map(partial(contact_rows, first_res=first_res, second=second), grouped)  24 us
    gather x1, local copies, waits for them, and re-layouts, later_rows(): jnp.take(following, jnp.maximum(row_ids - frame_rows, 0), axis=0)  20.1 us
    gather x1, local copies, waits for them, and re-layouts, later_rows(): own_part = jnp.take(own, jnp.minimum(row_ids, frame_rows - 1), axis=0)  19.9 us
  transfers between devices with their start and end apart: 4, of which 3 were waited for; matrix products, arithmetic and copies ran while one was open for 5% of the time, Pallas kernels for 0%

profile of v1, /device:TPU:0, one launch (start us, length us, event | category | flops | bytes accessed | tf_op | source)
XLA Modules:
  0.0 787.0 jit_solution(13970666713779171730)
XLA Ops:
  7.2 363.3 %while.2 = (s32[]{:T(128)}, bf16[4,128,8192]{2,1,0:T(8,128)(2,1)}, s32[8192]{0:T(1024)}, f32[4,128,3,384]{3,1,0,2:T(8,128)}, s32[64]{0:T(128)}, /*index=5*/s32[]{:T(128)}) while((s32[]{:T(128)}, bf16[4,128,8192]{2,1,0:T(8,128)(2,1)}, s32[8192]{0:T(1024)}, f32[4,128,3,384]{3,1,0,2:T(8,128)}, s32[64]{0:T(128)}, /*index=5*/s32[]{:T(128)}) %tuple.40), condition=%wide.region_2.3_spmd, body=%wide.region_0.2_spmd.sunk | while | flops 17933888 | bytes 85054936 | solution.py:39
  9.4 0.8 compare_select_fusion.6
  10.2 1.1 constant_dynamic-slice_fusion.2
  12.5 59.9 %gather_fusion = f32[8192,128,3]{1,2,0:T(4,128)} fusion(f32[128,3,384]{0,1,2:T(4,128)S(1)} %bitcast.55, s32[8192]{0:T(1024)S(1)} %broadcast_clamp_fusion.2), kind=kCustom, calls=%fused_computation.clone.1 | custom fusion | bytes 25198592 | tf_op jit(solution)/shard_map/while/body/eval_jaxpr/jit(_take)/gather | solution.py:27
  72.4 11.1 %copy.28 = f32[128,3,8192]{0,2,1:T(8,128)} copy(f32[128,3,8192]{0,1,2:T(4,128)} %bitcast.56) | data formatting | bytes 25165824 | tf_op jit(solution)/shard_map/while/body/eval_jaxpr/jit(_take)/gather | solution.py:27
  83.5 6.6 multiply_reduce_fusion.2
  90.1 2.0 divide_convert_fusion.2
  92.1 2.9 copy.30
  95.0 3.1 constant_dynamic-update-slice_fusion.2
  100.3 0.8 compare_select_fusion.6
  101.1 1.1 constant_dynamic-slice_fusion.2
  103.3 59.9 %gather_fusion = f32[8192,128,3]{1,2,0:T(4,128)} fusion(f32[128,3,384]{0,1,2:T(4,128)S(1)} %bitcast.55, s32[8192]{0:T(1024)S(1)} %broadcast_clamp_fusion.2), kind=kCustom, calls=%fused_computation.clone.1 | custom fusion | bytes 25198592 | tf_op jit(solution)/shard_map/while/body/eval_jaxpr/jit(_take)/gather | solution.py:27
  163.2 11.1 %copy.28 = f32[128,3,8192]{0,2,1:T(8,128)} copy(f32[128,3,8192]{0,1,2:T(4,128)} %bitcast.56) | data formatting | bytes 25165824 | tf_op jit(solution)/shard_map/while/body/eval_jaxpr/jit(_take)/gather | solution.py:27
  174.3 6.6 multiply_reduce_fusion.2
  180.9 2.0 divide_convert_fusion.2
  183.0 2.9 copy.30
  185.9 3.1 constant_dynamic-update-slice_fusion.2
  191.0 0.8 compare_select_fusion.6
  191.9 1.1 constant_dynamic-slice_fusion.2
  194.1 59.9 %gather_fusion = f32[8192,128,3]{1,2,0:T(4,128)} fusion(f32[128,3,384]{0,1,2:T(4,128)S(1)} %bitcast.55, s32[8192]{0:T(1024)S(1)} %broadcast_clamp_fusion.2), kind=kCustom, calls=%fused_computation.clone.1 | custom fusion | bytes 25198592 | tf_op jit(solution)/shard_map/while/body/eval_jaxpr/jit(_take)/gather | solution.py:27
  254.0 11.1 %copy.28 = f32[128,3,8192]{0,2,1:T(8,128)} copy(f32[128,3,8192]{0,1,2:T(4,128)} %bitcast.56) | data formatting | bytes 25165824 | tf_op jit(solution)/shard_map/while/body/eval_jaxpr/jit(_take)/gather | solution.py:27
  265.1 6.6 multiply_reduce_fusion.2
  271.7 2.0 divide_convert_fusion.2
  273.7 2.9 copy.30
  276.6 3.1 constant_dynamic-update-slice_fusion.2
  282.7 1.1 constant_dynamic-slice_fusion.2
  284.9 59.9 %gather_fusion = f32[8192,128,3]{1,2,0:T(4,128)} fusion(f32[128,3,384]{0,1,2:T(4,128)S(1)} %bitcast.55, s32[8192]{0:T(1024)S(1)} %broadcast_clamp_fusion.2), kind=kCustom, calls=%fused_computation.clone.1 | custom fusion | bytes 25198592 | tf_op jit(solution)/shard_map/while/body/eval_jaxpr/jit(_take)/gather | solution.py:27
  344.8 11.1 %copy.28 = f32[128,3,8192]{0,2,1:T(8,128)} copy(f32[128,3,8192]{0,1,2:T(4,128)} %bitcast.56) | data formatting | bytes 25165824 | tf_op jit(solution)/shard_map/while/body/eval_jaxpr/jit(_take)/gather | solution.py:27
  355.9 6.6 multiply_reduce_fusion.2
  362.5 2.0 divide_convert_fusion.2
  364.6 2.9 copy.30
  367.5 3.1 constant_dynamic-update-slice_fusion.2
  370.5 1.3 collective-permute-start
  371.8 6.9 convolution_bitcast_fusion.1
  379.8 19.9 %gather_fusion.2 = bf16[512,8192]{1,0:T(8,128)(2,1)} fusion(bf16[512,8192]{1,0:T(8,128)(2,1)} %bitcast.60, s32[1024]{0:T(1024)S(1)} %pad_clamp_fusion.2), kind=kCustom, calls=%fused_computation.2.clone | custom fusion | bytes 16779264 | tf_op jit(solution)/shard_map/while/body/eval_jaxpr/jit(_take)/gather | solution.py:44
  399.7 142.4 %all-reduce.4.cloned.1.call-done = f32[64,512]{1,0:T(8,128)} async-done(((f32[64,512]{1,0:T(8,128)}), f32[64,512]{1,0:T(8,128)}) %all-reduce.4.cloned.1.call-update) | async-done | bytes 131088 | tf_op jit(solution)/shard_map/psum | solution.py:59
  542.2 9.1 %fusion.9 = f32[512,8192]{1,0:T(8,128)} fusion(bf16[64,8192]{1,0:T(8,128)(2,1)S(1)} %copy-done, f32[64,512]{1,0:T(8,128)} %all-reduce.4.cloned.1.call-done, f32[64]{0:T(128)S(1)} %copy-done.4), kind=kOutput, calls=%fused_computation.39 | convolution fusion | flops 536936448 | bytes 17957120 | tf_op jit(solution)/shard_map/while/body/eval_jaxpr/dot_general | solution.py:72
  551.2 20.1 %gather_fusion.3 = bf16[512,8192]{1,0:T(8,128)(2,1)} fusion(bf16[512,8192]{1,0:T(8,128)(2,1)} %collective-permute-done, s32[1024]{0:T(1024)S(1)} %pad_clamp_fusion.1), kind=kCustom, calls=%fused_computation.3.clone | custom fusion | bytes 16779264 | tf_op jit(solution)/shard_map/while/body/eval_jaxpr/jit(_take)/gather | solution.py:45
  571.4 14.2 %select_convert_fusion = bf16[512,8192]{1,0:T(8,128)(2,1)S(1)} fusion(f32[512,8192]{1,0:T(8,128)} %fusion.9, bf16[512,8192]{1,0:T(8,128)(2,1)} %gather_fusion.3, bf16[512,8192]{1,0:T(8,128)(2,1)} %gather_fusion.2, f32[]{:T(128)S(6)} %sqrt.15, f32[8192]{0:T(1024)S(1)} %copy-done.3, pred[512]{0:T(512)(128)(4,1)S(1)} %get-tuple-element.89, ...), kind=kLoop, calls=%fused_computation.18 | loop fusion | flops 37748736 | bytes 41977860 | tf_op jit(solution)/shard_map/while/body/eval_jaxpr/convert_element_type | solution.py:80
  585.6 3.2 copy-done.1
  588.8 3.3 convolution_bitcast_fusion
  592.4 6.3 fusion.7
  598.8 37.8 %all-gather.3.cloned.1.call-done = f32[512,512]{1,0:T(8,128)} async-done(((f32[64,512]{1,0:T(8,128)}), f32[512,512]{1,0:T(8,128)}) %all-gather.3.cloned.1.call-update) | async-done | bytes 1048592 | tf_op jit(solution)/shard_map/all_gather | solution.py:13
  636.5 1.3 reduce_sum.18
  637.8 6.3 fusion.2
  644.2 130.1 %all-reduce.6.cloned.1.call-done = (f32[64,8192]{1,0:T(8,128)}, f32[64,8192]{1,0:T(8,128)}) async-done(((f32[64,8192]{1,0:T(8,128)}, f32[64,8192]{1,0:T(8,128)}), (f32[64,8192]{1,0:T(8,128)}, f32[64,8192]{1,0:T(8,128)})) %all-reduce.6.cloned.1.call-update) | async-done | bytes 4194320 | tf_op jit(solution)/shard_map/psum | solution.py:93
  774.3 3.1 copy.44
  777.4 3.1 copy.45
  (60 shorter events, 14.4 us)
Async XLA Ops:
  7.2 535.0 %copy-start = (bf16[64,8192]{1,0:T(8,128)(2,1)S(1)}, bf16[64,8192]{1,0:T(8,128)(2,1)}, u32[]{:S(2)}) copy-start(bf16[64,8192]{1,0:T(8,128)(2,1)} %param.17) | copy-start | bytes 3145732
  7.2 535.0 %all-reduce.4.cloned.1.call-start = ((), (), s32[]{:S(2)}) async-start(), calls=%async_computation | async-start | bytes 262144 | tf_op jit(solution)/shard_map/psum | solution.py:59
  370.5 180.7 %collective-permute-start = (bf16[512,8192]{1,0:T(8,128)(2,1)}, bf16[512,8192]{1,0:T(8,128)(2,1)}, u32[]{:S(2)}, u32[]{:S(2)}) collective-permute-start(bf16[512,8192]{1,0:T(8,128)(2,1)} %bitcast.58), channel_id=1, source_target_pairs={{8,0},{16,8},{24,16},{32,24},{40,32},{48,40},{56,48},{64,56},{72,6... | collective-permute-start | bytes 25165832 | tf_op jit(solution)/shard_map/ppermute | solution.py:22
  378.8 257.7 %all-gather.3.cloned.1.call-start = ((), (), s32[]{:S(2)}) async-start(), calls=%async_computation.1 | async-start | bytes 1179648 | tf_op jit(solution)/shard_map/all_gather | solution.py:13
  379.8 162.4 %copy-start.4 = (f32[64]{0:T(128)S(1)}, f32[64]{0:T(128)}, u32[]{:S(2)}) copy-start(f32[64]{0:T(128)} %param.16) | copy-start | bytes 772
  551.2 20.1 %copy-start.3 = (f32[8192]{0:T(1024)S(1)}, f32[8192]{0:T(1024)}, u32[]{:S(2)}) copy-start(f32[8192]{0:T(1024)} %param.18) | copy-start | bytes 98308
  585.5 3.2 copy-start.1
  588.8 3.7 copy-start.2
  592.1 182.2 %all-reduce.6.cloned.1.call-start = ((), (), s32[]{:S(2)}) async-start(), calls=%async_computation.2 | async-start | bytes 8388608 | tf_op jit(solution)/shard_map/psum | solution.py:93
Sparse Core Ops, SparseCore 0:
  378.9 163.2 all-reduce.3
  592.2 44.2 all-gather.2
  644.3 129.9 all-reduce.5
